TPU v7x, 256 devices: a whole 4x4x8 slice. The times are simulated.
256 devices in a mesh: dist: 16 (over z_lo, y), rows: 16 (over z_hi, x, core).
Axes of the slice: x: 4, y: 4, z: 8 (z_hi: 2, z_lo: 4; z = z_hi * 4 + z_lo), core: 2. Of those that a mesh axis runs over, the one named last changes fastest.
Arguments:
- wave: float32 [16, 2, 2048, 2048], P('dist', None, 'rows'), may hold values from -6 to 6
- object_slice: float32 [2, 2048, 2048], P(None, 'rows', 'dist'), may hold values from 0 to 1.5
- fresnel: float32 [16], P('dist'), may hold values from 256 to 1024
Outputs:
- detected: float32 [16, 2, 2048, 2048], P('dist', None, 'rows')
All inputs are finite; a program needn't handle non-finite values.
Results may differ from a plain program's by a relative error of at most 0.00035.
Values sent between devices are 32-bit elements; how exact they have to be, the bound alone decides.
A program may use at most 64 MiB of HBM per device.

v0:
```python
import math

import jax
import jax.numpy as jnp
from jax import lax
from jax.sharding import PartitionSpec as P

highest = lax.Precision.HIGHEST


def swapped(shard, axis, apart):
    return lax.ppermute(shard, axis, [(i, i ^ 1 << apart) for i in range(lax.axis_size(axis))])


def angle_table(period, direction, row_count, col_count):
    row_grid = lax.broadcasted_iota(jnp.int32, (row_count, col_count), 0)
    col_grid = lax.broadcasted_iota(jnp.int32, (row_count, col_count), 1)
    phase_angle = (
        direction * 2.0 * math.pi / period * (row_grid * col_grid % period).astype(jnp.float32)
    )
    return (jnp.cos(phase_angle), jnp.sin(phase_angle))


def complex_mix(form, real_part, imag_part, table_re, table_im):
    out_re = jnp.einsum(form, real_part, table_re, precision=highest) - jnp.einsum(
        form, imag_part, table_im, precision=highest
    )
    out_im = jnp.einsum(form, real_part, table_im, precision=highest) + jnp.einsum(
        form, imag_part, table_re, precision=highest
    )
    return (out_re, out_im)


def split_length(length):
    levels = length.bit_length() - 1
    outer_len = 1 << (levels + 1) // 2
    return (outer_len, length // outer_len)


def transform_last(real_part, imag_part, direction):
    length = real_part.shape[-1]
    outer_len, inner_len = split_length(length)
    leading = real_part.shape[:-1]
    real_part = real_part.reshape(leading + (outer_len, inner_len))
    imag_part = imag_part.reshape(leading + (outer_len, inner_len))
    first_re, first_im = angle_table(outer_len, direction, outer_len, outer_len)
    real_part, imag_part = complex_mix("...ab,ae->...eb", real_part, imag_part, first_re, first_im)
    twiddle_re, twiddle_im = angle_table(length, direction, outer_len, inner_len)
    real_part, imag_part = (
        real_part * twiddle_re - imag_part * twiddle_im,
        real_part * twiddle_im + imag_part * twiddle_re,
    )
    last_re, last_im = angle_table(inner_len, direction, inner_len, inner_len)
    real_part, imag_part = complex_mix("...eb,bd->...de", real_part, imag_part, last_re, last_im)
    return (real_part.reshape(leading + (length,)), imag_part.reshape(leading + (length,)))


def signed_frequency(index_line, length):
    return (
        jnp.where(index_line < length // 2, index_line, index_line - length).astype(jnp.float32)
        / length
    )


def apply_kernel(real_part, imag_part, fresnel, row_index, col_index, length):
    row_freq = signed_frequency(row_index, length)
    col_freq = signed_frequency(col_index, length)
    freq_sum = row_freq[:, None] ** 2 + col_freq[None, :] ** 2
    phase_angle = (-math.pi * fresnel)[:, None, None] * freq_sum[None]
    kernel_re = jnp.cos(phase_angle)
    kernel_im = jnp.sin(phase_angle)
    return (
        real_part * kernel_re - imag_part * kernel_im,
        real_part * kernel_im + imag_part * kernel_re,
    )


def body(wave, object_slice, fresnel):
    row_count = wave.shape[2]
    length = wave.shape[3]
    group_size = lax.axis_size("rows")
    position = lax.axis_index("rows")
    slice_piece = lax.all_gather(object_slice, "dist", axis=2, tiled=True)
    amplitude = jnp.exp(-slice_piece[1])
    trans_re = amplitude * jnp.cos(slice_piece[0])
    trans_im = amplitude * jnp.sin(slice_piece[0])
    wave_re = wave[:, 0]
    wave_im = wave[:, 1]
    exited = jnp.stack(
        (wave_re * trans_re - wave_im * trans_im, wave_re * trans_im + wave_im * trans_re), axis=1
    )
    real_part, imag_part = transform_last(exited[:, 0], exited[:, 1], -1.0)
    rounds = group_size.bit_length() - 1
    for level in reversed(range(rounds)):
        stride = 1 << level
        partner = swapped(jnp.stack((real_part, imag_part), axis=1), "rows", level)
        upper_flag = (position // stride % 2).astype(jnp.float32)
        within = (position % stride).astype(jnp.float32)
        phase_angle = -2.0 * math.pi / (2 * stride) * within
        factor_re = 1.0 - upper_flag + upper_flag * jnp.cos(phase_angle)
        factor_im = upper_flag * jnp.sin(phase_angle)
        own_sign = 1.0 - 2.0 * upper_flag
        summed_re = partner[:, 0] + own_sign * real_part
        summed_im = partner[:, 1] + own_sign * imag_part
        real_part = summed_re * factor_re - summed_im * factor_im
        imag_part = summed_re * factor_im + summed_im * factor_re
    bit_reverse = jnp.zeros((), jnp.int32)
    for level in range(rounds):
        bit_reverse = bit_reverse + position // (1 << level) % 2 * (1 << rounds - 1 - level)
    local_rows = lax.iota(jnp.int32, row_count)
    shift_angle = -2.0 * math.pi / length * (local_rows * bit_reverse % length).astype(jnp.float32)
    shift_re = jnp.cos(shift_angle)[:, None]
    shift_im = jnp.sin(shift_angle)[:, None]
    real_part, imag_part = (
        real_part * shift_re - imag_part * shift_im,
        real_part * shift_im + imag_part * shift_re,
    )
    local_re, local_im = angle_table(row_count, -1.0, row_count, row_count)
    real_part, imag_part = complex_mix("...lc,lm->...mc", real_part, imag_part, local_re, local_im)
    row_index = bit_reverse + group_size * local_rows
    col_index = lax.iota(jnp.int32, length)
    real_part, imag_part = apply_kernel(real_part, imag_part, fresnel, row_index, col_index, length)
    back_re, back_im = angle_table(row_count, 1.0, row_count, row_count)
    real_part, imag_part = complex_mix("...lc,lm->...mc", real_part, imag_part, back_re, back_im)
    real_part = real_part / row_count
    imag_part = imag_part / row_count
    real_part, imag_part = (
        real_part * shift_re + imag_part * shift_im,
        imag_part * shift_re - real_part * shift_im,
    )
    for level in range(rounds):
        stride = 1 << level
        partner = swapped(jnp.stack((real_part, imag_part), axis=1), "rows", level)
        upper_flag = (position // stride % 2).astype(jnp.float32)
        within = (position % stride).astype(jnp.float32)
        phase_angle = 2.0 * math.pi / (2 * stride) * within
        turn_re = jnp.cos(phase_angle)
        turn_im = jnp.sin(phase_angle)
        lower_flag = 1.0 - upper_flag
        second_re = upper_flag * real_part + lower_flag * partner[:, 0]
        second_im = upper_flag * imag_part + lower_flag * partner[:, 1]
        first_re = upper_flag * partner[:, 0] + lower_flag * real_part
        first_im = upper_flag * partner[:, 1] + lower_flag * imag_part
        turned_re = second_re * turn_re - second_im * turn_im
        turned_im = second_re * turn_im + second_im * turn_re
        own_sign = 1.0 - 2.0 * upper_flag
        real_part = 0.5 * (first_re + own_sign * turned_re)
        imag_part = 0.5 * (first_im + own_sign * turned_im)
    real_part, imag_part = transform_last(real_part, imag_part, 1.0)
    real_part = real_part / length
    imag_part = imag_part / length
    return jnp.stack((real_part, imag_part), axis=1)


def solution(mesh):
    return jax.shard_map(
        body,
        mesh=mesh,
        in_specs=(P("dist", None, "rows", None), P(None, "rows", "dist"), P("dist")),
        out_specs=P("dist", None, "rows", None),
        check_vma=False,
    )
```

profile of v0, /device:TPU:97, one launch (start us, length us, event | category | flops | bytes accessed | tf_op | source)
XLA Modules:
  0.0 554.5 jit_solution(11762353641238578681)
XLA Ops:
  6.5 1.7 copy.21
  8.3 1.7 fusion.252
  10.7 67.3 %all-gather.2.cloned.1.call-done = f32[2,128,2048]{1,2,0:T(8,128)} async-done(((f32[2,128,128]{1,2,0:T(8,128)}), f32[2,128,2048]{1,2,0:T(8,128)}) %all-gather.2.cloned.1.call-update) | async-done | bytes 2097168 | tf_op jit(solution)/shard_map/all_gather | solution.py:83
  78.0 5.1 fusion.24
  83.1 1.7 fusion.47
  84.7 1.6 fusion.49
  86.4 1.7 fusion.8
  88.0 2.2 add_bitcast_fusion.1
  90.2 1.6 fusion.41
  91.8 1.6 fusion.43
  93.4 2.6 broadcast_multiply_fusion
  96.0 1.7 copy.32
  97.8 1.6 copy.34
  99.4 2.7 broadcast_multiply_fusion.1
  103.0 1.5 pad_maximum_fusion
  104.4 4.2 collective-permute-start
  108.7 88.3 %collective-permute-done = f32[1,2,128,2048]{3,2,1,0:T(8,128)} collective-permute-done((f32[1,2,128,2048]{3,2,1,0:T(8,128)}, f32[1,2,128,2048]{3,2,1,0:T(8,128)}, u32[]{:S(2)}, u32[]{:S(2)}) %collective-permute-start) | collective-permute-done | bytes 2097184 | tf_op jit(solution)/shard_map/ppermute | solution.py:12
  197.0 1.9 multiply_add_fusion.10
  199.1 0.8 copy-done
  199.9 2.6 collective-permute-start.1
  202.7 40.7 %collective-permute-done.1 = f32[1,2,128,2048]{3,2,1,0:T(8,128)} collective-permute-done((f32[1,2,128,2048]{3,2,1,0:T(8,128)S(1)}, f32[1,2,128,2048]{3,2,1,0:T(8,128)}, u32[]{:S(2)}, u32[]{:S(2)}) %collective-permute-start.1) | collective-permute-done | bytes 2097184 | tf_op jit(solution)/shard_map/ppermute | solution.py:12
  243.5 2.3 multiply_add_fusion.7
  245.7 1.5 pad_maximum_fusion.2
  247.2 1.2 collective-permute-start.2
  248.6 39.9 %collective-permute-done.2 = f32[1,2,128,2048]{3,2,1,0:T(8,128)} collective-permute-done((f32[1,2,128,2048]{3,2,1,0:T(8,128)}, f32[1,2,128,2048]{3,2,1,0:T(8,128)}, u32[]{:S(2)}, u32[]{:S(2)}) %collective-permute-start.2) | collective-permute-done | bytes 2097184 | tf_op jit(solution)/shard_map/ppermute | solution.py:12
  288.5 1.9 multiply_subtract_fusion.4
  290.5 1.5 pad_maximum_fusion.3
  292.0 7.2 %collective-permute-start.3 = (f32[1,2,128,2048]{3,2,1,0:T(8,128)}, f32[1,2,128,2048]{3,2,1,0:T(8,128)}, u32[]{:S(2)}, u32[]{:S(2)}) collective-permute-start(f32[1,2,128,2048]{3,2,1,0:T(8,128)} %pad_maximum_fusion.3), channel_id=1, source_target_pairs={{0,1},{1,0},{2,3},{3,2},{4,5},{5,4},{6,7},{7,6},{8,9},{9,8},{10,11... | collective-permute-start | bytes 6291464 | tf_op jit(solution)/shard_map/ppermute | solution.py:12
  302.2 2.8 bitcast_add_fusion.20
  305.0 2.4 fusion.11
  307.4 1.4 fusion.10
  308.9 1.5 fusion.58
  310.4 1.5 fusion.59
  312.0 1.5 convolution_subtract_fusion.1
  313.5 1.5 convolution_add_fusion.1
  315.1 5.5 fusion.57
  320.6 5.0 fusion.56
  325.6 5.2 convolution_subtract_fusion
  330.8 5.3 multiply_add_fusion
  336.4 4.1 collective-permute-done.4
  340.5 0.9 multiply_bitcast_fusion.5
  341.4 1.5 pad_maximum_fusion.5
  342.9 1.2 collective-permute-start.5
  344.3 46.0 %collective-permute-done.5 = f32[1,2,128,2048]{3,2,1,0:T(8,128)} collective-permute-done((f32[1,2,128,2048]{3,2,1,0:T(8,128)}, f32[1,2,128,2048]{3,2,1,0:T(8,128)}, u32[]{:S(2)}, u32[]{:S(2)}) %collective-permute-start.5) | collective-permute-done | bytes 2097184 | tf_op jit(solution)/shard_map/ppermute | solution.py:12
  390.3 3.4 multiply_bitcast_fusion.3
  393.7 1.5 pad_maximum_fusion.6
  395.2 2.7 collective-permute-start.6
  398.0 45.1 %collective-permute-done.6 = f32[1,2,128,2048]{3,2,1,0:T(8,128)S(1)} collective-permute-done((f32[1,2,128,2048]{3,2,1,0:T(8,128)}, f32[1,2,128,2048]{3,2,1,0:T(8,128)S(1)}, u32[]{:S(2)}, u32[]{:S(2)}) %collective-permute-start.6) | collective-permute-done | bytes 2097184 | tf_op jit(solution)/shard_map/ppermute | solution.py:12
  443.1 1.3 copy-done.3
  444.4 2.7 multiply_bitcast_fusion.1
  447.1 1.5 pad_maximum_fusion.7
  448.5 3.6 collective-permute-start.7
  452.4 70.4 %collective-permute-done.7 = f32[1,2,128,2048]{3,2,1,0:T(8,128)} collective-permute-done((f32[1,2,128,2048]{3,2,1,0:T(8,128)}, f32[1,2,128,2048]{3,2,1,0:T(8,128)}, u32[]{:S(2)}, u32[]{:S(2)}) %collective-permute-start.7) | collective-permute-done | bytes 2097184 | tf_op jit(solution)/shard_map/ppermute | solution.py:12
  522.8 3.3 fusion.14
  526.1 1.5 copy.41
  527.7 2.6 fusion.37
  530.3 1.7 fusion.35
  532.3 2.9 fusion.5
  535.2 2.1 add_bitcast_fusion
  537.3 1.6 fusion.31
  539.0 1.6 fusion.29
  540.6 1.8 fusion.3
  543.0 1.6 fusion.1
  545.4 1.8 copy.53
  (30 shorter events, 6.3 us)
Async XLA Ops:
  6.5 71.5 %all-gather.2.cloned.1.call-start = ((), (), s32[]{:S(2)}) async-start(), calls=%async_computation | async-start | bytes 2228224 | tf_op jit(solution)/shard_map/all_gather | solution.py:83
  104.4 92.6 %collective-permute-start = (f32[1,2,128,2048]{3,2,1,0:T(8,128)}, f32[1,2,128,2048]{3,2,1,0:T(8,128)}, u32[]{:S(2)}, u32[]{:S(2)}) collective-permute-start(f32[1,2,128,2048]{3,2,1,0:T(8,128)} %pad_maximum_fusion), channel_id=1, source_target_pairs={{0,8},{1,9},{2,10},{3,11},{4,12},{5,13},{6,14},{7,15},{8,0},{9,1},... | collective-permute-start | bytes 6291464 | tf_op jit(solution)/shard_map/ppermute | solution.py:12
  198.9 1.0 copy-start
  199.9 43.5 %collective-permute-start.1 = (f32[1,2,128,2048]{3,2,1,0:T(8,128)S(1)}, f32[1,2,128,2048]{3,2,1,0:T(8,128)}, u32[]{:S(2)}, u32[]{:S(2)}) collective-permute-start(f32[1,2,128,2048]{3,2,1,0:T(8,128)S(1)} %pad_maximum_fusion.1), channel_id=1, source_target_pairs={{0,4},{1,5},{2,6},{3,7},{4,0},{5,1},{6,2},{7,3},{8,12},{9,13},{10,... | collective-permute-start | bytes 6291464 | tf_op jit(solution)/shard_map/ppermute | solution.py:12
  247.2 41.3 %collective-permute-start.2 = (f32[1,2,128,2048]{3,2,1,0:T(8,128)}, f32[1,2,128,2048]{3,2,1,0:T(8,128)}, u32[]{:S(2)}, u32[]{:S(2)}) collective-permute-start(f32[1,2,128,2048]{3,2,1,0:T(8,128)} %pad_maximum_fusion.2), channel_id=1, source_target_pairs={{0,2},{1,3},{2,0},{3,1},{4,6},{5,7},{6,4},{7,5},{8,10},{9,11},{10,... | collective-permute-start | bytes 6291464 | tf_op jit(solution)/shard_map/ppermute | solution.py:12
  290.5 9.5 %copy-start.1 = (f32[1,128,32,64]{1,2,3,0:T(8,128)S(1)}, f32[1,128,32,64]{1,2,3,0:T(8,128)}, u32[]{:S(2)}) copy-start(f32[1,128,32,64]{1,2,3,0:T(8,128)} %get-tuple-element.48) | copy-start | bytes 3145732
  292.0 13.1 %collective-permute-start.3 = (f32[1,2,128,2048]{3,2,1,0:T(8,128)}, f32[1,2,128,2048]{3,2,1,0:T(8,128)}, u32[]{:S(2)}, u32[]{:S(2)}) collective-permute-start(f32[1,2,128,2048]{3,2,1,0:T(8,128)} %pad_maximum_fusion.3), channel_id=1, source_target_pairs={{0,1},{1,0},{2,3},{3,2},{4,5},{5,4},{6,7},{7,6},{8,9},{9,8},{10,11... | collective-permute-start | bytes 6291464 | tf_op jit(solution)/shard_map/ppermute | solution.py:12
  300.0 1.2 copy-start.2
  336.3 4.2 collective-permute-start.4
  342.9 47.4 %collective-permute-start.5 = (f32[1,2,128,2048]{3,2,1,0:T(8,128)}, f32[1,2,128,2048]{3,2,1,0:T(8,128)}, u32[]{:S(2)}, u32[]{:S(2)}) collective-permute-start(f32[1,2,128,2048]{3,2,1,0:T(8,128)} %pad_maximum_fusion.5), channel_id=1, source_target_pairs={{0,2},{1,3},{2,0},{3,1},{4,6},{5,7},{6,4},{7,5},{8,10},{9,11},{10,... | collective-permute-start | bytes 6291464 | tf_op jit(solution)/shard_map/ppermute | solution.py:12
  395.2 47.9 %collective-permute-start.6 = (f32[1,2,128,2048]{3,2,1,0:T(8,128)}, f32[1,2,128,2048]{3,2,1,0:T(8,128)S(1)}, u32[]{:S(2)}, u32[]{:S(2)}) collective-permute-start(f32[1,2,128,2048]{3,2,1,0:T(8,128)} %pad_maximum_fusion.6), channel_id=1, source_target_pairs={{0,4},{1,5},{2,6},{3,7},{4,0},{5,1},{6,2},{7,3},{8,12},{9,13},{10,... | collective-permute-start | bytes 6291464 | tf_op jit(solution)/shard_map/ppermute | solution.py:12
  443.1 1.3 copy-start.3
  448.5 74.2 %collective-permute-start.7 = (f32[1,2,128,2048]{3,2,1,0:T(8,128)}, f32[1,2,128,2048]{3,2,1,0:T(8,128)}, u32[]{:S(2)}, u32[]{:S(2)}) collective-permute-start(f32[1,2,128,2048]{3,2,1,0:T(8,128)} %pad_maximum_fusion.7), channel_id=1, source_target_pairs={{0,8},{1,9},{2,10},{3,11},{4,12},{5,13},{6,14},{7,15},{8,0},{9,1},... | collective-permute-start | bytes 6291464 | tf_op jit(solution)/shard_map/ppermute | solution.py:12
Sparse Core Ops, SparseCore 0:
  9.1 68.7 all-gather.1
where the time goes:
time: 565 us; the launch traced here: 555 us
  waiting for transfers between devices  402 us (71%)
  matrix products  58.6 us (10%)
  other arithmetic  37.9 us (7%)
  starting transfers between devices  22.9 us (4%)
  local copies, waits for them, and re-layouts  17.4 us (3%)
  between operations  15.9 us (3%)
    ppermute x8, waiting for transfers between devices, swapped(): lax.ppermute(shard, axis, [(i, i ^ 1 << apart) for i in range(lax.axis_si...  334 us
    all_gather x1, waiting for transfers between devices, body(): slice_piece = lax.all_gather(object_slice, 'dist', axis=2, tiled=True)  67.3 us
    ppermute x8, starting transfers between devices, swapped(): lax.ppermute(shard, axis, [(i, i ^ 1 << apart) for i in range(lax.axis_si...  22.9 us
    dot_general x6, matrix products, complex_mix(): jnp.einsum(form, imag_part, table_im, precision=highest)  16.3 us
    another operation x11, other arithmetic, body(): partner = swapped(jnp.stack((real_part, imag_part), axis=1), 'rows', level)  16.2 us
    dot_general x6, matrix products, complex_mix(): jnp.einsum(form, imag_part, table_re, precision=highest)  14.8 us
    dot_general x6, matrix products, complex_mix(): jnp.einsum(form, real_part, table_re, precision=highest)  14 us
    dot_general x6, matrix products, complex_mix(): jnp.einsum(form, real_part, table_im, precision=highest)  13.5 us
  transfers between devices with their start and end apart: 9, of which 8 were waited for; matrix products, arithmetic and copies ran while one was open for 1% of the time, Pallas kernels for 0%

commit v1 on v0

v1 whole, which is shorter than its diff:
```python
import functools
import math

import jax
import jax.numpy as jnp
from jax import lax
from jax.experimental import pallas as pl
from jax.experimental.pallas import tpu as pltpu
from jax.sharding import PartitionSpec as P

F32 = jnp.float32
BF16 = jnp.bfloat16
LANES = 128
BLOCKS = 16
LENGTH = LANES * BLOCKS
CHUNKS = 4
ROWS = LANES // CHUNKS
SUB = 16


def dft4(points, direction):
    (ar, ai), (br, bi), (cr, ci), (dr, di) = points
    er, ei, fr, fi = ar + cr, ai + ci, ar - cr, ai - ci
    gr, gi, hr, hi = br + dr, bi + di, br - dr, bi - di
    plus, minus = (fr - hi, fi + hr), (fr + hi, fi - hr)
    if direction < 0:
        plus, minus = minus, plus
    return [(er + gr, ei + gi), plus, (er - gr, ei - gi), minus]


def turned(point, steps, direction):
    re, im = point
    steps %= 16
    if steps == 0:
        return point
    if steps == 4:
        return (-im, re) if direction > 0 else (im, -re)
    angle = direction * 2.0 * math.pi * steps / 16
    turn_re, turn_im = math.cos(angle), math.sin(angle)
    if steps == 2:
        return ((re - direction * im) * turn_re, (im + direction * re) * turn_re)
    return (re * turn_re - im * turn_im, re * turn_im + im * turn_re)


def dft16(points, direction):
    inner = [dft4([points[4 * a1 + a0] for a1 in range(4)], direction) for a0 in range(4)]
    out = [None] * 16
    for q0 in range(4):
        column = [turned(inner[a0][q0], a0 * q0, direction) for a0 in range(4)]
        for q1, value in enumerate(dft4(column, direction)):
            out[q0 + 4 * q1] = value
    return out


def halves(value):
    high = value.astype(BF16)
    return high, (value - high.astype(F32)).astype(BF16)


def build_matrices(fresnel, line_ref, s_hi, s_lo):
    q1 = lax.broadcasted_iota(jnp.int32, (BLOCKS, LANES), 0)
    q2 = lax.broadcasted_iota(jnp.int32, (BLOCKS, LANES), 1)
    index = q1 + BLOCKS * q2
    signed = jnp.where(index < LENGTH // 2, index, index - LENGTH).astype(F32)
    turns = fresnel * (signed * signed) * (1.0 / (LENGTH * LENGTH))
    turns = turns - 2.0 * jnp.floor(turns * 0.5 + 0.5)
    phase = -math.pi * turns
    phase_re, phase_im = jnp.cos(phase), jnp.sin(phase)
    row = lax.broadcasted_iota(jnp.int32, (LANES, LANES), 0)
    col = lax.broadcasted_iota(jnp.int32, (LANES, LANES), 1)
    angle = (2.0 * math.pi / LANES) * ((row * col) % LANES).astype(F32)
    table_re, table_im = jnp.cos(angle) * (1.0 / LENGTH), jnp.sin(angle) * (1.0 / LENGTH)
    dot = functools.partial(jnp.dot, precision=lax.Precision.HIGHEST, preferred_element_type=F32)
    line_re = dot(phase_re, table_re) - dot(phase_im, table_im)
    line_im = dot(phase_re, table_im) + dot(phase_im, table_re)
    twist = (2.0 * math.pi / LENGTH) * (q1 * q2).astype(F32)
    twist_re, twist_im = jnp.cos(twist), jnp.sin(twist)
    line_re, line_im = (
        line_re * twist_re - line_im * twist_im,
        line_re * twist_im + line_im * twist_re,
    )
    wrap = (-2.0 * math.pi / BLOCKS) * q1.astype(F32)
    wrap_re, wrap_im = jnp.cos(wrap), jnp.sin(wrap)
    line_ref[0] = line_re
    line_ref[1] = line_im
    line_ref[2] = line_re * wrap_re - line_im * wrap_im
    line_ref[3] = line_re * wrap_im + line_im * wrap_re
    ahead = col >= row

    def one(k, carry):
        def spread(part):
            line = jnp.broadcast_to(line_ref[part, pl.ds(k, 1), :], (LANES, LANES))
            return pltpu.roll(line, 0, 1, stride=1, stride_axis=0)

        re_hi, re_lo = halves(jnp.where(ahead, spread(0), spread(2)))
        im_hi, im_lo = halves(jnp.where(ahead, spread(1), spread(3)))
        for target, re, im in ((s_hi, re_hi, im_hi), (s_lo, re_lo, im_lo)):
            target[k, :LANES, :LANES] = re
            target[k, :LANES, LANES:] = im
            target[k, LANES:, :LANES] = -im
            target[k, LANES:, LANES:] = re
        return carry

    lax.fori_loop(0, BLOCKS, one, 0)


def kernel(
    fresnel_ref, slice_ref, wave_hbm, out_hbm,
    wave, trans, sent, taken, back, line_ref, s_hi, s_lo, lhs, mid, rhs, mid_row,
    wave_sem, z_send, z_recv, y_send, y_recv, go_send, go_recv, back_send, back_recv,
):
    me = lax.axis_index("rows")
    spot = lax.axis_index("dist")
    z_hi, x, core = me // 8, (me // 2) % 4, me % 2
    z_lo, y = spot // 4, spot % 4
    fetch = pltpu.make_async_copy(wave_hbm, wave, wave_sem)
    fetch.start()
    z_peers = [{"dist": (z_lo + k) % 4 * 4 + y, "rows": me} for k in (1, 3, 2)]
    y_peers = [{"dist": z_lo * 4 + (y + k) % 4, "rows": me} for k in (1, 3, 2)]
    row_peers = []
    for far, dx, other in [(f, a, c) for f in (1, 0) for a in (0, 1, 3, 2) for c in (0, 1)]:
        if (far, dx, other) != (0, 0, 0):
            row_peers.append((z_hi + far) % 2 * 8 + (x + dx) % 4 * 2 + (core + other) % 2)

    barrier = pltpu.get_barrier_semaphore()
    peers = z_peers + y_peers + [{"dist": spot, "rows": p} for p in row_peers]
    for peer in peers:
        pl.semaphore_signal(barrier, inc=1, device_id=peer)

    def transmission(g, carry):
        rows = pl.ds(pl.multiple_of(g * ROWS, ROWS), ROWS)
        amplitude = jnp.exp(-slice_ref[1, rows, :])
        trans[g, y, z_lo, 0] = amplitude * jnp.cos(slice_ref[0, rows, :])
        trans[g, y, z_lo, 1] = amplitude * jnp.sin(slice_ref[0, rows, :])
        return carry

    lax.fori_loop(0, CHUNKS, transmission, 0)
    pl.semaphore_wait(barrier, len(peers))

    def z_copies(g):
        own = trans.at[g, y, z_lo]
        return [
            pltpu.make_async_remote_copy(own, own, z_send.at[g], z_recv.at[g], device_id=peer)
            for peer in z_peers
        ]

    def y_copies(g):
        own = trans.at[g, y]
        return [
            pltpu.make_async_remote_copy(own, own, y_send.at[g], y_recv.at[g], device_id=peer)
            for peer in y_peers
        ]

    def z_start(g, carry):
        for copy in z_copies(g):
            copy.start()
        return carry

    lax.fori_loop(0, CHUNKS, z_start, 0)

    def pass_on(g):
        held = trans.at[g, 0, pl.ds(0, 3)]
        pltpu.make_async_copy(held, held, z_recv.at[g]).wait()
        for copy in y_copies(g):
            copy.start()

    pass_on(0)
    build_matrices(fresnel_ref[0], line_ref, s_hi, s_lo)
    fetch.wait()

    def exchange(outbox, target, g, send_sem, recv_sem):
        for p in row_peers:
            pltpu.make_async_remote_copy(
                outbox.at[g, p], target, send_sem.at[g], recv_sem,
                device_id={"dist": spot, "rows": p},
            ).start()
        pltpu.make_async_copy(outbox.at[g, me], target, recv_sem).start()

    def column_part(g, carry):
        @pl.when(g + 1 < CHUNKS)
        def _():
            pass_on(g + 1)

        held = trans.at[g, pl.ds(0, 3)]
        pltpu.make_async_copy(held, held, y_recv.at[g]).wait()

        def forward(j, carry):
            here = pl.ds(pl.multiple_of(j * SUB, SUB), SUB)
            there = pl.ds(pl.multiple_of(g * ROWS + j * SUB, SUB), SUB)
            low = pl.ds(pl.multiple_of(ROWS + j * SUB, SUB), SUB)
            points = []
            for a in range(BLOCKS):
                wave_re = wave[0, there, a * LANES : (a + 1) * LANES]
                wave_im = wave[1, there, a * LANES : (a + 1) * LANES]
                turn_re = trans[g, a % 4, a // 4, 0, here, :]
                turn_im = trans[g, a % 4, a // 4, 1, here, :]
                points.append(
                    (wave_re * turn_re - wave_im * turn_im, wave_re * turn_im + wave_im * turn_re)
                )
            for q, (re, im) in enumerate(dft16(points, -1)):
                re_hi, re_lo = halves(re)
                im_hi, im_lo = halves(im)
                lhs[q, here, :LANES] = re_hi
                lhs[q, here, LANES:] = im_hi
                lhs[q, low, :LANES] = re_lo
                lhs[q, low, LANES:] = im_lo
            return carry

        lax.fori_loop(0, ROWS // SUB, forward, 0)

        def multiply(q, carry):
            both = jnp.dot(lhs[q], s_hi[q], preferred_element_type=F32)
            rest = jnp.dot(lhs[q, :ROWS, :], s_lo[q], preferred_element_type=F32)
            mid[q] = both[:ROWS] + (both[ROWS:] + rest)
            return carry

        lax.fori_loop(0, BLOCKS, multiply, 0, unroll=4)

        def inverse(j, carry):
            here = pl.ds(pl.multiple_of(j * SUB, SUB), SUB)
            points = [(mid[q, here, :LANES], mid[q, here, LANES:]) for q in range(BLOCKS)]
            for a, (re, im) in enumerate(dft16(points, 1)):
                sent[g, a, 0, here, :] = re
                sent[g, a, 1, here, :] = im
            return carry

        lax.fori_loop(0, ROWS // SUB, inverse, 0)
        exchange(sent, taken.at[g, me], g, go_send, go_recv.at[g])
        return carry

    lax.fori_loop(0, CHUNKS, column_part, 0)

    def row_forward(g, carry):
        pltpu.make_async_copy(taken.at[g], taken.at[g], go_recv.at[g]).wait()

        def forward(j, carry):
            here = pl.ds(pl.multiple_of(j * SUB, SUB), SUB)
            re_rows = pl.ds(pl.multiple_of(g * ROWS + j * SUB, SUB), SUB)
            im_rows = pl.ds(pl.multiple_of(LANES + g * ROWS + j * SUB, SUB), SUB)
            points = [(taken[g, a, 0, here, :], taken[g, a, 1, here, :]) for a in range(BLOCKS)]
            for q, (re, im) in enumerate(dft16(points, -1)):
                re_hi, re_lo = halves(re)
                im_hi, im_lo = halves(-im)
                rhs[q, re_rows, :LANES] = re_hi
                rhs[q, re_rows, LANES:] = re_lo
                rhs[q, im_rows, :LANES] = im_hi
                rhs[q, im_rows, LANES:] = im_lo
            return carry

        return lax.fori_loop(0, ROWS // SUB, forward, carry)

    lax.fori_loop(0, CHUNKS, row_forward, 0)

    def row_multiply(q, carry):
        turn = (BLOCKS - q) % BLOCKS
        both = jnp.dot(s_hi[turn], rhs[q], preferred_element_type=F32)
        rest = jnp.dot(s_lo[turn], rhs[q, :, :LANES], preferred_element_type=F32)
        mid_row[q] = both[:, :LANES] + (both[:, LANES:] + rest)
        return carry

    lax.fori_loop(0, BLOCKS, row_multiply, 0, unroll=4)

    def row_inverse(g, carry):
        def inverse(j, carry):
            here = pl.ds(pl.multiple_of(j * SUB, SUB), SUB)
            re_rows = pl.ds(pl.multiple_of(g * ROWS + j * SUB, SUB), SUB)
            im_rows = pl.ds(pl.multiple_of(LANES + g * ROWS + j * SUB, SUB), SUB)
            points = [(mid_row[q, re_rows, :], -mid_row[q, im_rows, :]) for q in range(BLOCKS)]
            for a, (re, im) in enumerate(dft16(points, 1)):
                back[g, a, 0, here, :] = re
                back[g, a, 1, here, :] = im
            return carry

        lax.fori_loop(0, ROWS // SUB, inverse, 0)
        rows = pl.ds(pl.multiple_of(g * ROWS, ROWS), ROWS)
        cols = pl.ds(pl.multiple_of(me * LANES, LANES), LANES)
        exchange(back, out_hbm.at[:, rows, cols], g, back_send, back_recv)
        return carry

    lax.fori_loop(0, CHUNKS, row_inverse, 0)

    def settle(g, carry):
        for copy in z_copies(g):
            copy.wait_send()
        for copy in y_copies(g):
            copy.wait_send()
        some = sent.at[g, pl.ds(0, BLOCKS - 1)]
        pltpu.make_async_copy(some, some, go_send.at[g]).wait()
        pltpu.make_async_copy(some, some, back_send.at[g]).wait()
        return carry

    lax.fori_loop(0, CHUNKS, settle, 0)
    pltpu.make_async_copy(out_hbm, out_hbm, back_recv).wait()


def body(wave, object_slice, fresnel):
    box = (CHUNKS, BLOCKS, 2, ROWS, LANES)
    dma = pltpu.SemaphoreType.DMA
    out = pl.pallas_call(
        kernel,
        out_shape=jax.ShapeDtypeStruct((2, LANES, LENGTH), F32),
        in_specs=[
            pl.BlockSpec(memory_space=pltpu.SMEM),
            pl.BlockSpec(memory_space=pltpu.VMEM),
            pl.BlockSpec(memory_space=pl.ANY),
        ],
        out_specs=pl.BlockSpec(memory_space=pl.ANY),
        scratch_shapes=[
            pltpu.VMEM((2, LANES, LENGTH), F32),
            pltpu.VMEM((CHUNKS, 4, 4, 2, ROWS, LANES), F32),
            pltpu.VMEM(box, F32),
            pltpu.VMEM(box, F32),
            pltpu.VMEM(box, F32),
            pltpu.VMEM((4, BLOCKS, LANES), F32),
            pltpu.VMEM((BLOCKS, 2 * LANES, 2 * LANES), BF16),
            pltpu.VMEM((BLOCKS, 2 * LANES, 2 * LANES), BF16),
            pltpu.VMEM((BLOCKS, 2 * ROWS, 2 * LANES), BF16),
            pltpu.VMEM((BLOCKS, ROWS, 2 * LANES), F32),
            pltpu.VMEM((BLOCKS, 2 * LANES, 2 * LANES), BF16),
            pltpu.VMEM((BLOCKS, 2 * LANES, LANES), F32),
            dma, dma((CHUNKS,)), dma((CHUNKS,)), dma((CHUNKS,)), dma((CHUNKS,)),
            dma((CHUNKS,)), dma((CHUNKS,)), dma((CHUNKS,)), dma,
        ],
        compiler_params=pltpu.CompilerParams(
            collective_id=0, has_side_effects=True, vmem_limit_bytes=48 << 20
        ),
        name="propagate",
    )(fresnel, object_slice, wave[0])
    return out[None]


def solution(mesh):
    return jax.shard_map(
        body,
        mesh=mesh,
        in_specs=(P("dist", None, "rows", None), P(None, "rows", "dist"), P("dist")),
        out_specs=P("dist", None, "rows", None),
        check_vma=False,
    )
```

time: 565 us -> 139 us (0.25)
  the two profiles are of different devices: /device:TPU:97 before, /device:TPU:1 now
where the time goes in v1:
time: 139 us; the launch traced here: 138 us
  Pallas kernels  133 us (96%)
  local copies, waits for them, and re-layouts  3.81 us (3%)
    pallas_call x1, Pallas kernels, body(): pl.pallas_call(kernel, out_shape=jax.ShapeDtypeStruct((2, LANES, LENGTH),...  133 us
    unnamed x5, local copies, waits for them, and re-layouts  3.81 us

profile of v1, /device:TPU:1, one launch (start us, length us, event | category | flops | bytes accessed | tf_op | source)
XLA Modules:
  0.0 138.0 jit_solution(12150926825902594090)
XLA Ops:
  0.7 0.0 copy-start
  0.7 1.6 %copy-done = f32[1,2,128,2048]{3,2,1,0:T(8,128)S(1)} copy-done((f32[1,2,128,2048]{3,2,1,0:T(8,128)S(1)}, f32[1,2,128,2048]{3,2,1,0:T(8,128)}, u32[]{:S(2)}) %copy-start) | copy-done | bytes 2097176
  2.2 0.0 copy-start.1
  2.2 0.9 copy-done.1
  3.1 133.5 %propagate.1 = f32[2,128,2048]{2,1,0:T(8,128)S(1)} custom-call(f32[1]{0:T(128)S(6)} %copy.5.fresnel_ref, f32[2,128,128]{2,1,0:T(8,128)S(1)} %copy-done.1, f32[2,128,2048]{2,1,0:T(8,128)S(1)} %bitcast.3), custom_call_target="tpu_custom_call" | custom-call | tf_op jit(solution)/shard_map/propagate/pallas_call | solution.py:299
  136.6 1.3 copy.6
Async XLA Ops:
  0.7 1.6 %copy-start = (f32[1,2,128,2048]{3,2,1,0:T(8,128)S(1)}, f32[1,2,128,2048]{3,2,1,0:T(8,128)}, u32[]{:S(2)}) copy-start(f32[1,2,128,2048]{3,2,1,0:T(8,128)} %param.3) | copy-start | bytes 6291460
  2.2 0.9 copy-start.1

commit v2 on v1

v2 whole, which is shorter than its diff:
```python
import functools
import math

import jax
import jax.numpy as jnp
from jax import lax
from jax.experimental import pallas as pl
from jax.experimental.pallas import tpu as pltpu
from jax.sharding import PartitionSpec as P

F32 = jnp.float32
BF16 = jnp.bfloat16
LANES = 128
BLOCKS = 16
LENGTH = LANES * BLOCKS
SUB = 16
GO = ((0, 16), (16, 16), (32, 32), (64, 64))
BACK = ((0, 32), (32, 96))


def dft4(points, direction):
    (ar, ai), (br, bi), (cr, ci), (dr, di) = points
    er, ei, fr, fi = ar + cr, ai + ci, ar - cr, ai - ci
    gr, gi, hr, hi = br + dr, bi + di, br - dr, bi - di
    plus, minus = (fr - hi, fi + hr), (fr + hi, fi - hr)
    if direction < 0:
        plus, minus = minus, plus
    return [(er + gr, ei + gi), plus, (er - gr, ei - gi), minus]


def turned(point, steps, direction):
    re, im = point
    steps %= 16
    if steps == 0:
        return point
    if steps == 4:
        return (-im, re) if direction > 0 else (im, -re)
    angle = direction * 2.0 * math.pi * steps / 16
    turn_re, turn_im = math.cos(angle), math.sin(angle)
    if steps == 2:
        return ((re - direction * im) * turn_re, (im + direction * re) * turn_re)
    return (re * turn_re - im * turn_im, re * turn_im + im * turn_re)


def dft16(points, direction):
    inner = [dft4([points[4 * a1 + a0] for a1 in range(4)], direction) for a0 in range(4)]
    out = [None] * 16
    for q0 in range(4):
        column = [turned(inner[a0][q0], a0 * q0, direction) for a0 in range(4)]
        for q1, value in enumerate(dft4(column, direction)):
            out[q0 + 4 * q1] = value
    return out


def halves(value):
    high = value.astype(BF16)
    return high, (value - high.astype(F32)).astype(BF16)


def build_matrices(fresnel, line_ref, s_hi, s_lo):
    q1 = lax.broadcasted_iota(jnp.int32, (BLOCKS, LANES), 0)
    q2 = lax.broadcasted_iota(jnp.int32, (BLOCKS, LANES), 1)
    index = q1 + BLOCKS * q2
    signed = jnp.where(index < LENGTH // 2, index, index - LENGTH).astype(F32)
    turns = fresnel * (signed * signed) * (1.0 / (LENGTH * LENGTH))
    turns = turns - 2.0 * jnp.floor(turns * 0.5 + 0.5)
    phase = -math.pi * turns
    phase_re, phase_im = jnp.cos(phase), jnp.sin(phase)
    row = lax.broadcasted_iota(jnp.int32, (LANES, LANES), 0)
    col = lax.broadcasted_iota(jnp.int32, (LANES, LANES), 1)
    angle = (2.0 * math.pi / LANES) * ((row * col) % LANES).astype(F32)
    table_re, table_im = jnp.cos(angle) * (1.0 / LENGTH), jnp.sin(angle) * (1.0 / LENGTH)
    dot = functools.partial(jnp.dot, precision=lax.Precision.HIGHEST, preferred_element_type=F32)
    line_re = dot(phase_re, table_re) - dot(phase_im, table_im)
    line_im = dot(phase_re, table_im) + dot(phase_im, table_re)
    twist = (2.0 * math.pi / LENGTH) * (q1 * q2).astype(F32)
    twist_re, twist_im = jnp.cos(twist), jnp.sin(twist)
    line_re, line_im = (
        line_re * twist_re - line_im * twist_im,
        line_re * twist_im + line_im * twist_re,
    )
    wrap = (-2.0 * math.pi / BLOCKS) * q1.astype(F32)
    wrap_re, wrap_im = jnp.cos(wrap), jnp.sin(wrap)
    line_ref[0] = line_re
    line_ref[1] = line_im
    line_ref[2] = line_re * wrap_re - line_im * wrap_im
    line_ref[3] = line_re * wrap_im + line_im * wrap_re
    ahead = col >= row

    def one(k, carry):
        def spread(part):
            line = jnp.broadcast_to(line_ref[part, pl.ds(k, 1), :], (LANES, LANES))
            return pltpu.roll(line, 0, 1, stride=1, stride_axis=0)

        re_hi, re_lo = halves(jnp.where(ahead, spread(0), spread(2)))
        im_hi, im_lo = halves(jnp.where(ahead, spread(1), spread(3)))
        for target, re, im in ((s_hi, re_hi, im_hi), (s_lo, re_lo, im_lo)):
            target[k, :LANES, :LANES] = re
            target[k, :LANES, LANES:] = im
            target[k, LANES:, :LANES] = -im
            target[k, LANES:, LANES:] = re
        return carry

    lax.fori_loop(0, BLOCKS, one, 0)


def kernel(
    fresnel_ref, slice_hbm, wave_hbm, out_hbm,
    piece, wave, trans, sent, taken, back, line_ref, s_hi, s_lo, lhs, mid, rhs, mid_row,
    slice_sem, wave_sem, z_send, z_recv, y_send, y_recv, go_send, go_recv, back_send, back_recv,
):
    me = lax.axis_index("rows")
    spot = lax.axis_index("dist")
    z_hi, x, core = me // 8, (me // 2) % 4, me % 2
    z_lo, y = spot // 4, spot % 4
    fetch_slice = pltpu.make_async_copy(slice_hbm, piece, slice_sem)
    fetch_slice.start()
    fetch = pltpu.make_async_copy(wave_hbm, wave, wave_sem)
    fetch.start()
    z_peers = [{"dist": (z_lo + k) % 4 * 4 + y, "rows": me} for k in (1, 3, 2)]
    y_peers = [{"dist": z_lo * 4 + (y + k) % 4, "rows": me} for k in (1, 3, 2)]
    row_peers = []
    for far, dx, other in [(f, a, c) for f in (1, 0) for a in (0, 1, 3, 2) for c in (0, 1)]:
        if (far, dx, other) != (0, 0, 0):
            row_peers.append((z_hi + far) % 2 * 8 + (x + dx) % 4 * 2 + (core + other) % 2)

    barrier = pltpu.get_barrier_semaphore()
    peers = z_peers + y_peers + [{"dist": spot, "rows": p} for p in row_peers]
    for peer in peers:
        pl.semaphore_signal(barrier, inc=1, device_id=peer)

    fetch_slice.wait()

    def transmission(j, carry):
        rows = pl.ds(pl.multiple_of(j * SUB, SUB), SUB)
        amplitude = jnp.exp(-piece[1, rows, :])
        trans[y, z_lo, 0, rows, :] = amplitude * jnp.cos(piece[0, rows, :])
        trans[y, z_lo, 1, rows, :] = amplitude * jnp.sin(piece[0, rows, :])
        return carry

    lax.fori_loop(0, LANES // SUB, transmission, 0)
    pl.semaphore_wait(barrier, len(peers))

    def z_copies(g):
        own = trans.at[y, z_lo, :, pl.ds(*GO[g])]
        return [
            pltpu.make_async_remote_copy(own, own, z_send.at[g], z_recv.at[g], device_id=peer)
            for peer in z_peers
        ]

    def y_copies(g):
        own = trans.at[y, :, :, pl.ds(*GO[g])]
        return [
            pltpu.make_async_remote_copy(own, own, y_send.at[g], y_recv.at[g], device_id=peer)
            for peer in y_peers
        ]

    def settled(view, sem):
        pltpu.make_async_copy(view, view, sem).wait()

    def pass_on(g):
        settled(trans.at[0, pl.ds(0, 3), :, pl.ds(*GO[g])], z_recv.at[g])
        for copy in y_copies(g):
            copy.start()

    def exchange(outbox, rows, target, send_sem, recv_sem):
        for p in row_peers:
            pltpu.make_async_remote_copy(
                outbox.at[p, :, rows], target, send_sem, recv_sem,
                device_id={"dist": spot, "rows": p},
            ).start()
        pltpu.make_async_copy(outbox.at[me, :, rows], target, recv_sem).start()

    def column_part(first, count):
        def forward(j, carry):
            here = pl.ds(pl.multiple_of(j * SUB, SUB), SUB)
            low = pl.ds(pl.multiple_of(count + j * SUB, SUB), SUB)
            there = pl.ds(pl.multiple_of(first + j * SUB, SUB), SUB)
            points = []
            for a in range(BLOCKS):
                wave_re = wave[0, there, a * LANES : (a + 1) * LANES]
                wave_im = wave[1, there, a * LANES : (a + 1) * LANES]
                turn_re = trans[a % 4, a // 4, 0, there, :]
                turn_im = trans[a % 4, a // 4, 1, there, :]
                points.append(
                    (wave_re * turn_re - wave_im * turn_im, wave_re * turn_im + wave_im * turn_re)
                )
            for q, (re, im) in enumerate(dft16(points, -1)):
                re_hi, re_lo = halves(re)
                im_hi, im_lo = halves(im)
                lhs[q, here, :LANES] = re_hi
                lhs[q, here, LANES:] = im_hi
                lhs[q, low, :LANES] = re_lo
                lhs[q, low, LANES:] = im_lo
            return carry

        lax.fori_loop(0, count // SUB, forward, 0)

        def multiply(q, carry):
            both = jnp.dot(lhs[q, : 2 * count, :], s_hi[q], preferred_element_type=F32)
            rest = jnp.dot(lhs[q, :count, :], s_lo[q], preferred_element_type=F32)
            mid[q, :count, :] = both[:count] + (both[count:] + rest)
            return carry

        lax.fori_loop(0, BLOCKS, multiply, 0, unroll=4)

        def inverse(j, carry):
            here = pl.ds(pl.multiple_of(j * SUB, SUB), SUB)
            there = pl.ds(pl.multiple_of(first + j * SUB, SUB), SUB)
            points = [(mid[q, here, :LANES], mid[q, here, LANES:]) for q in range(BLOCKS)]
            for a, (re, im) in enumerate(dft16(points, 1)):
                sent[a, 0, there, :] = re
                sent[a, 1, there, :] = im
            return carry

        lax.fori_loop(0, count // SUB, inverse, 0)

    for g in range(len(GO)):
        for copy in z_copies(g):
            copy.start()
    for g in range(len(GO)):
        pass_on(g)
    build_matrices(fresnel_ref[0], line_ref, s_hi, s_lo)
    fetch.wait()
    for g, (first, count) in enumerate(GO):
        rows = pl.ds(first, count)
        settled(trans.at[pl.ds(0, 3), :, :, rows], y_recv.at[g])
        column_part(first, count)
        exchange(sent, rows, taken.at[me, :, rows], go_send.at[g], go_recv.at[g])

    def row_forward(j, carry):
        here = pl.ds(pl.multiple_of(j * SUB, SUB), SUB)
        im_rows = pl.ds(pl.multiple_of(LANES + j * SUB, SUB), SUB)
        points = [(taken[a, 0, here, :], taken[a, 1, here, :]) for a in range(BLOCKS)]
        for q, (re, im) in enumerate(dft16(points, -1)):
            re_hi, re_lo = halves(re)
            im_hi, im_lo = halves(-im)
            rhs[q, here, :LANES] = re_hi
            rhs[q, here, LANES:] = re_lo
            rhs[q, im_rows, :LANES] = im_hi
            rhs[q, im_rows, LANES:] = im_lo
        return carry

    for g, (first, count) in enumerate(GO):
        settled(taken.at[:, :, pl.ds(first, count)], go_recv.at[g])
        lax.fori_loop(first // SUB, (first + count) // SUB, row_forward, 0)

    def row_multiply(q, carry):
        turn = (BLOCKS - q) % BLOCKS
        both = jnp.dot(s_hi[turn], rhs[q], preferred_element_type=F32)
        rest = jnp.dot(s_lo[turn], rhs[q, :, :LANES], preferred_element_type=F32)
        mid_row[q] = both[:, :LANES] + (both[:, LANES:] + rest)
        return carry

    lax.fori_loop(0, BLOCKS, row_multiply, 0, unroll=4)

    def row_inverse(j, carry):
        here = pl.ds(pl.multiple_of(j * SUB, SUB), SUB)
        im_rows = pl.ds(pl.multiple_of(LANES + j * SUB, SUB), SUB)
        points = [(mid_row[q, here, :], -mid_row[q, im_rows, :]) for q in range(BLOCKS)]
        for a, (re, im) in enumerate(dft16(points, 1)):
            back[a, 0, here, :] = re
            back[a, 1, here, :] = im
        return carry

    cols = pl.ds(pl.multiple_of(me * LANES, LANES), LANES)
    for g, (first, count) in enumerate(BACK):
        lax.fori_loop(first // SUB, (first + count) // SUB, row_inverse, 0)
        rows = pl.ds(first, count)
        exchange(back, rows, out_hbm.at[:, rows, cols], back_send.at[g], back_recv)

    for g, (first, count) in enumerate(GO):
        for copy in z_copies(g) + y_copies(g):
            copy.wait_send()
        settled(sent.at[pl.ds(0, BLOCKS - 1), :, pl.ds(first, count)], go_send.at[g])
    for g, (first, count) in enumerate(BACK):
        settled(back.at[pl.ds(0, BLOCKS - 1), :, pl.ds(first, count)], back_send.at[g])
    settled(out_hbm, back_recv)


def body(wave, object_slice, fresnel):
    box = pltpu.VMEM((BLOCKS, 2, LANES, LANES), F32)
    matrices = pltpu.VMEM((BLOCKS, 2 * LANES, 2 * LANES), BF16)
    most = max(count for _, count in GO)
    dma = pltpu.SemaphoreType.DMA
    go = dma((len(GO),))
    out = pl.pallas_call(
        kernel,
        out_shape=jax.ShapeDtypeStruct((2, LANES, LENGTH), F32),
        in_specs=[
            pl.BlockSpec(memory_space=pltpu.SMEM),
            pl.BlockSpec(memory_space=pl.ANY),
            pl.BlockSpec(memory_space=pl.ANY),
        ],
        out_specs=pl.BlockSpec(memory_space=pl.ANY),
        scratch_shapes=[
            pltpu.VMEM((2, LANES, LANES), F32),
            pltpu.VMEM((2, LANES, LENGTH), F32),
            pltpu.VMEM((4, 4, 2, LANES, LANES), F32),
            box, box, box,
            pltpu.VMEM((4, BLOCKS, LANES), F32),
            matrices, matrices,
            pltpu.VMEM((BLOCKS, 2 * most, 2 * LANES), BF16),
            pltpu.VMEM((BLOCKS, most, 2 * LANES), F32),
            matrices,
            pltpu.VMEM((BLOCKS, 2 * LANES, LANES), F32),
            dma, dma, go, go, go, go, go, go, dma((len(BACK),)), dma,
        ],
        compiler_params=pltpu.CompilerParams(
            collective_id=0, has_side_effects=True, vmem_limit_bytes=60 << 20
        ),
        name="propagate",
    )(fresnel, object_slice, wave[0])
    return out[None]


def solution(mesh):
    return jax.shard_map(
        body,
        mesh=mesh,
        in_specs=(P("dist", None, "rows", None), P(None, "rows", "dist"), P("dist")),
        out_specs=P("dist", None, "rows", None),
        check_vma=False,
    )
```

time: 139 us -> 128 us (0.921)
  Pallas kernels: 133 us -> 124 us
    pallas_call x1, Pallas kernels: 133 us -> 124 us  [body(): pl.pallas_call(kernel, out_shape=jax.ShapeDtypeStruct((2, LANES, LENGTH),...]
    unnamed x5 -> x1, local copies, waits for them, and re-layouts: 3.81 us -> 3.14 us
where the time goes in v2:
time: 128 us
  Pallas kernels  124 us (97%)
  local copies, waits for them, and re-layouts  3.14 us (2%)
    pallas_call x1, Pallas kernels, body(): pl.pallas_call(kernel, out_shape=jax.ShapeDtypeStruct((2, LANES, LENGTH),...  124 us
    unnamed x1, local copies, waits for them, and re-layouts  3.14 us

profile of v2, /device:TPU:1, one launch (start us, length us, event | category | flops | bytes accessed | tf_op | source)
XLA Modules:
  0.0 127.9 jit_solution(7506762119915285315)
XLA Ops:
  0.7 124.1 %propagate.1 = f32[2,128,2048]{2,1,0:T(8,128)} custom-call(f32[1]{0:T(128)S(6)} %copy.5.fresnel_ref, f32[2,128,128]{2,1,0:T(8,128)} %slice_hbm.1, f32[2,128,2048]{2,1,0:T(8,128)} %bitcast.3), custom_call_target="tpu_custom_call" | custom-call | tf_op jit(solution)/shard_map/propagate/pallas_call | solution.py:287
  124.8 3.1 %copy.6 = f32[1,2,128,2048]{3,2,1,0:T(8,128)} copy(f32[1,2,128,2048]{3,2,1,0:T(8,128)} %bitcast.2) | data formatting | bytes 4194304

commit v3 on v2

--- a/solution.py
+++ b/solution.py
@@ -14,8 +14,8 @@
 BLOCKS = 16
 LENGTH = LANES * BLOCKS
 SUB = 16
-GO = ((0, 16), (16, 16), (32, 32), (64, 64))
-BACK = ((0, 32), (32, 96))
+GO = ((0, 32), (32, 32), (64, 64),)
+BACK = ((0, 32), (32, 32), (64, 64),)
 
 
 def dft4(points, direction):
@@ -105,16 +105,14 @@
 
 
 def kernel(
-    fresnel_ref, slice_hbm, wave_hbm, out_hbm,
-    piece, wave, trans, sent, taken, back, line_ref, s_hi, s_lo, lhs, mid, rhs, mid_row,
-    slice_sem, wave_sem, z_send, z_recv, y_send, y_recv, go_send, go_recv, back_send, back_recv,
+    fresnel_ref, piece, wave_hbm, out_hbm,
+    wave, trans, sent, taken, back, line_ref, s_hi, s_lo, lhs, mid, rhs, mid_row,
+    wave_sem, z_send, z_recv, y_send, y_recv, go_send, go_recv, back_send, back_recv, answer,
 ):
     me = lax.axis_index("rows")
     spot = lax.axis_index("dist")
     z_hi, x, core = me // 8, (me // 2) % 4, me % 2
     z_lo, y = spot // 4, spot % 4
-    fetch_slice = pltpu.make_async_copy(slice_hbm, piece, slice_sem)
-    fetch_slice.start()
     fetch = pltpu.make_async_copy(wave_hbm, wave, wave_sem)
     fetch.start()
     z_peers = [{"dist": (z_lo + k) % 4 * 4 + y, "rows": me} for k in (1, 3, 2)]
@@ -125,11 +123,15 @@
             row_peers.append((z_hi + far) % 2 * 8 + (x + dx) % 4 * 2 + (core + other) % 2)
 
     barrier = pltpu.get_barrier_semaphore()
-    peers = z_peers + y_peers + [{"dist": spot, "rows": p} for p in row_peers]
+    far_peers = [{"dist": spot, "rows": p} for p in row_peers[:8]]
+    peers = z_peers + y_peers + [{"dist": spot, "rows": p} for p in row_peers[8:]]
     for peer in peers:
         pl.semaphore_signal(barrier, inc=1, device_id=peer)
 
-    fetch_slice.wait()
+    @pl.when(z_hi == 0)
+    def _():
+        for peer in far_peers:
+            pl.semaphore_signal(barrier, inc=1, device_id=peer)
 
     def transmission(j, carry):
         rows = pl.ds(pl.multiple_of(j * SUB, SUB), SUB)
@@ -139,7 +141,12 @@
         return carry
 
     lax.fori_loop(0, LANES // SUB, transmission, 0)
-    pl.semaphore_wait(barrier, len(peers))
+    pl.semaphore_wait(barrier, len(peers) + len(far_peers) * z_hi)
+
+    @pl.when(z_hi == 1)
+    def _():
+        for peer in far_peers:
+            pl.semaphore_signal(answer, inc=1, device_id=peer)
 
     def z_copies(g):
         own = trans.at[y, z_lo, :, pl.ds(*GO[g])]
@@ -218,14 +225,20 @@
     for g in range(len(GO)):
         for copy in z_copies(g):
             copy.start()
+    build_matrices(fresnel_ref[0], line_ref, s_hi, s_lo)
     for g in range(len(GO)):
         pass_on(g)
-    build_matrices(fresnel_ref[0], line_ref, s_hi, s_lo)
     fetch.wait()
     for g, (first, count) in enumerate(GO):
         rows = pl.ds(first, count)
         settled(trans.at[pl.ds(0, 3), :, :, rows], y_recv.at[g])
         column_part(first, count)
+        if g == 0:
+
+            @pl.when(z_hi == 0)
+            def _():
+                pl.semaphore_wait(answer, len(far_peers))
+
         exchange(sent, rows, taken.at[me, :, rows], go_send.at[g], go_recv.at[g])
 
     def row_forward(j, carry):
@@ -289,12 +302,11 @@
         out_shape=jax.ShapeDtypeStruct((2, LANES, LENGTH), F32),
         in_specs=[
             pl.BlockSpec(memory_space=pltpu.SMEM),
-            pl.BlockSpec(memory_space=pl.ANY),
+            pl.BlockSpec(memory_space=pltpu.VMEM),
             pl.BlockSpec(memory_space=pl.ANY),
         ],
         out_specs=pl.BlockSpec(memory_space=pl.ANY),
         scratch_shapes=[
-            pltpu.VMEM((2, LANES, LANES), F32),
             pltpu.VMEM((2, LANES, LENGTH), F32),
             pltpu.VMEM((4, 4, 2, LANES, LANES), F32),
             box, box, box,
@@ -304,10 +316,11 @@
             pltpu.VMEM((BLOCKS, most, 2 * LANES), F32),
             matrices,
             pltpu.VMEM((BLOCKS, 2 * LANES, LANES), F32),
-            dma, dma, go, go, go, go, go, go, dma((len(BACK),)), dma,
+            dma, go, go, go, go, go, go, dma((len(BACK),)), dma,
+            pltpu.SemaphoreType.REGULAR,
         ],
         compiler_params=pltpu.CompilerParams(
-            collective_id=0, has_side_effects=True, vmem_limit_bytes=60 << 20
+            collective_id=0, has_side_effects=True, vmem_limit_bytes=50 << 20
         ),
         name="propagate",
     )(fresnel, object_slice, wave[0])

time: 128 us -> 123 us (0.961)
  Pallas kernels: 124 us -> 120 us
    pallas_call x1, Pallas kernels: 124 us -> 120 us  [body(): pl.pallas_call(kernel, out_shape=jax.ShapeDtypeStruct((2, LANES, LENGTH),...]
    unnamed x1 -> x3, local copies, waits for them, and re-layouts: 3.14 us -> 2.22 us
where the time goes in v3:
time: 123 us
  Pallas kernels  120 us (98%)
  local copies, waits for them, and re-layouts  2.22 us (2%)
    pallas_call x1, Pallas kernels, body(): pl.pallas_call(kernel, out_shape=jax.ShapeDtypeStruct((2, LANES, LENGTH),...  120 us

profile of v3, /device:TPU:1, one launch (start us, length us, event | category | flops | bytes accessed | tf_op | source)
XLA Modules:
  0.0 122.7 jit_solution(6384402200681477964)
XLA Ops:
  0.7 0.0 copy-start
  0.7 0.9 copy-done
  1.6 119.8 %propagate.1 = f32[2,128,2048]{2,1,0:T(8,128)S(1)} custom-call(f32[1]{0:T(128)S(6)} %copy.5.fresnel_ref, f32[2,128,128]{2,1,0:T(8,128)S(1)} %copy-done, f32[2,128,2048]{2,1,0:T(8,128)} %bitcast.3), custom_call_target="tpu_custom_call" | custom-call | tf_op jit(solution)/shard_map/propagate/pallas_call | solution.py:300
  121.3 1.3 %copy.6 = f32[1,2,128,2048]{3,2,1,0:T(8,128)} copy(f32[1,2,128,2048]{3,2,1,0:T(8,128)S(1)} %bitcast.2) | data formatting | bytes 4194304
Async XLA Ops:
  0.7 0.9 copy-start

commit v4 on v3

--- a/solution.py
+++ b/solution.py
@@ -105,14 +105,16 @@
 
 
 def kernel(
-    fresnel_ref, piece, wave_hbm, out_hbm,
-    wave, trans, sent, taken, back, line_ref, s_hi, s_lo, lhs, mid, rhs, mid_row,
-    wave_sem, z_send, z_recv, y_send, y_recv, go_send, go_recv, back_send, back_recv, answer,
+    fresnel_ref, slice_hbm, wave_hbm, out_hbm,
+    piece, wave, trans, sent, taken, back, line_ref, s_hi, s_lo, lhs, mid, rhs, mid_row,
+    slice_sem, wave_sem, z_send, z_recv, y_send, y_recv, go_send, go_recv, back_send, back_recv, answer, ready,
 ):
     me = lax.axis_index("rows")
     spot = lax.axis_index("dist")
     z_hi, x, core = me // 8, (me // 2) % 4, me % 2
     z_lo, y = spot // 4, spot % 4
+    fetch_slice = pltpu.make_async_copy(slice_hbm, piece, slice_sem)
+    fetch_slice.start()
     fetch = pltpu.make_async_copy(wave_hbm, wave, wave_sem)
     fetch.start()
     z_peers = [{"dist": (z_lo + k) % 4 * 4 + y, "rows": me} for k in (1, 3, 2)]
@@ -122,6 +124,7 @@
         if (far, dx, other) != (0, 0, 0):
             row_peers.append((z_hi + far) % 2 * 8 + (x + dx) % 4 * 2 + (core + other) % 2)
 
+    near_and_far = [p for pair in zip(row_peers[:7], row_peers[8:]) for p in pair] + row_peers[7:8]
     barrier = pltpu.get_barrier_semaphore()
     far_peers = [{"dist": spot, "rows": p} for p in row_peers[:8]]
     peers = z_peers + y_peers + [{"dist": spot, "rows": p} for p in row_peers[8:]]
@@ -132,6 +135,8 @@
     def _():
         for peer in far_peers:
             pl.semaphore_signal(barrier, inc=1, device_id=peer)
+
+    fetch_slice.wait()
 
     def transmission(j, carry):
         rows = pl.ds(pl.multiple_of(j * SUB, SUB), SUB)
@@ -169,9 +174,12 @@
         settled(trans.at[0, pl.ds(0, 3), :, pl.ds(*GO[g])], z_recv.at[g])
         for copy in y_copies(g):
             copy.start()
-
-    def exchange(outbox, rows, target, send_sem, recv_sem):
-        for p in row_peers:
+        if g + 1 == len(GO):
+            for peer in z_peers:
+                pl.semaphore_signal(ready, inc=1, device_id=peer)
+
+    def exchange(order, outbox, rows, target, send_sem, recv_sem):
+        for p in order:
             pltpu.make_async_remote_copy(
                 outbox.at[p, :, rows], target, send_sem, recv_sem,
                 device_id={"dist": spot, "rows": p},
@@ -234,12 +242,13 @@
         settled(trans.at[pl.ds(0, 3), :, :, rows], y_recv.at[g])
         column_part(first, count)
         if g == 0:
+            pl.semaphore_wait(ready, len(z_peers))
 
             @pl.when(z_hi == 0)
             def _():
                 pl.semaphore_wait(answer, len(far_peers))
 
-        exchange(sent, rows, taken.at[me, :, rows], go_send.at[g], go_recv.at[g])
+        exchange(near_and_far, sent, rows, taken.at[me, :, rows], go_send.at[g], go_recv.at[g])
 
     def row_forward(j, carry):
         here = pl.ds(pl.multiple_of(j * SUB, SUB), SUB)
@@ -280,7 +289,7 @@
     for g, (first, count) in enumerate(BACK):
         lax.fori_loop(first // SUB, (first + count) // SUB, row_inverse, 0)
         rows = pl.ds(first, count)
-        exchange(back, rows, out_hbm.at[:, rows, cols], back_send.at[g], back_recv)
+        exchange(row_peers, back, rows, out_hbm.at[:, rows, cols], back_send.at[g], back_recv)
 
     for g, (first, count) in enumerate(GO):
         for copy in z_copies(g) + y_copies(g):
@@ -302,11 +311,12 @@
         out_shape=jax.ShapeDtypeStruct((2, LANES, LENGTH), F32),
         in_specs=[
             pl.BlockSpec(memory_space=pltpu.SMEM),
-            pl.BlockSpec(memory_space=pltpu.VMEM),
+            pl.BlockSpec(memory_space=pl.ANY),
             pl.BlockSpec(memory_space=pl.ANY),
         ],
         out_specs=pl.BlockSpec(memory_space=pl.ANY),
         scratch_shapes=[
+            pltpu.VMEM((2, LANES, LANES), F32),
             pltpu.VMEM((2, LANES, LENGTH), F32),
             pltpu.VMEM((4, 4, 2, LANES, LANES), F32),
             box, box, box,
@@ -316,14 +326,14 @@
             pltpu.VMEM((BLOCKS, most, 2 * LANES), F32),
             matrices,
             pltpu.VMEM((BLOCKS, 2 * LANES, LANES), F32),
-            dma, go, go, go, go, go, go, dma((len(BACK),)), dma,
-            pltpu.SemaphoreType.REGULAR,
+            dma, dma, go, go, go, go, go, go, dma((len(BACK),)), dma,
+            pltpu.SemaphoreType.REGULAR, pltpu.SemaphoreType.REGULAR,
         ],
         compiler_params=pltpu.CompilerParams(
             collective_id=0, has_side_effects=True, vmem_limit_bytes=50 << 20
         ),
         name="propagate",
-    )(fresnel, object_slice, wave[0])
+    )(fresnel, *(pltpu.with_memory_space_constraint(a, pltpu.HBM) for a in (object_slice, wave[0])))
     return out[None]
 
 

time: 123 us -> 122 us (level)
  the two profiles are of different devices: /device:TPU:1 before, /device:TPU:130 now
where the time goes in v4:
time: 122 us
  Pallas kernels  120 us (98%)
  local copies, waits for them, and re-layouts  1.32 us (1%)
    pallas_call x1, Pallas kernels, body(): pl.pallas_call(kernel, out_shape=jax.ShapeDtypeStruct((2, LANES, LENGTH),...  120 us

profile of v4, /device:TPU:130, one launch (start us, length us, event | category | flops | bytes accessed | tf_op | source)
XLA Modules:
  0.0 121.7 jit_solution(17366668448509963226)
XLA Ops:
  0.7 119.7 %propagate.1 = f32[2,128,2048]{2,1,0:T(8,128)S(1)} custom-call(f32[1]{0:T(128)S(6)} %copy.5.fresnel_ref, f32[2,128,128]{2,1,0:T(8,128)} %slice_hbm.1, f32[2,128,2048]{2,1,0:T(8,128)} %bitcast.3), custom_call_target="tpu_custom_call" | custom-call | tf_op jit(solution)/shard_map/propagate/pallas_call | solution.py:309
  120.3 1.3 %copy.6 = f32[1,2,128,2048]{3,2,1,0:T(8,128)} copy(f32[1,2,128,2048]{3,2,1,0:T(8,128)S(1)} %bitcast.2) | data formatting | bytes 4194304

commit v5 on v4

--- a/solution.py
+++ b/solution.py
@@ -274,7 +274,7 @@
         mid_row[q] = both[:, :LANES] + (both[:, LANES:] + rest)
         return carry
 
-    lax.fori_loop(0, BLOCKS, row_multiply, 0, unroll=4)
+    lax.fori_loop(0, BLOCKS, row_multiply, 0, unroll=16)
 
     def row_inverse(j, carry):
         here = pl.ds(pl.multiple_of(j * SUB, SUB), SUB)

time: 122 us -> 121 us (level)
  no operation moved by 1% of the time
where the time goes in v5:
time: 121 us
  Pallas kernels  119 us (98%)
  local copies, waits for them, and re-layouts  1.32 us (1%)
    pallas_call x1, Pallas kernels, body(): pl.pallas_call(kernel, out_shape=jax.ShapeDtypeStruct((2, LANES, LENGTH),...  119 us

profile of v5, /device:TPU:130, one launch (start us, length us, event | category | flops | bytes accessed | tf_op | source)
XLA Modules:
  0.0 121.4 jit_solution(18046942887664015779)
XLA Ops:
  0.7 119.4 %propagate.1 = f32[2,128,2048]{2,1,0:T(8,128)S(1)} custom-call(f32[1]{0:T(128)S(6)} %copy.5.fresnel_ref, f32[2,128,128]{2,1,0:T(8,128)} %slice_hbm.1, f32[2,128,2048]{2,1,0:T(8,128)} %bitcast.3), custom_call_target="tpu_custom_call" | custom-call | tf_op jit(solution)/shard_map/propagate/pallas_call | solution.py:309
  120.1 1.3 %copy.6 = f32[1,2,128,2048]{3,2,1,0:T(8,128)} copy(f32[1,2,128,2048]{3,2,1,0:T(8,128)S(1)} %bitcast.2) | data formatting | bytes 4194304

commit v6 on v5

--- a/solution.py
+++ b/solution.py
@@ -217,7 +217,7 @@
             mid[q, :count, :] = both[:count] + (both[count:] + rest)
             return carry
 
-        lax.fori_loop(0, BLOCKS, multiply, 0, unroll=4)
+        lax.fori_loop(0, BLOCKS, multiply, 0, unroll=8)
 
         def inverse(j, carry):
             here = pl.ds(pl.multiple_of(j * SUB, SUB), SUB)

time: 121 us -> 122 us (level)
  the two profiles are of different devices: /device:TPU:130 before, /device:TPU:224 now
where the time goes in v6:
time: 122 us
  Pallas kernels  120 us (98%)
  local copies, waits for them, and re-layouts  1.32 us (1%)
    pallas_call x1, Pallas kernels, body(): pl.pallas_call(kernel, out_shape=jax.ShapeDtypeStruct((2, LANES, LENGTH),...  120 us

profile of v6, /device:TPU:224, one launch (start us, length us, event | category | flops | bytes accessed | tf_op | source)
XLA Modules:
  0.0 122.0 jit_solution(3072967633625843089)
XLA Ops:
  0.7 120.0 %propagate.1 = f32[2,128,2048]{2,1,0:T(8,128)S(1)} custom-call(f32[1]{0:T(128)S(6)} %copy.5.fresnel_ref, f32[2,128,128]{2,1,0:T(8,128)} %slice_hbm.1, f32[2,128,2048]{2,1,0:T(8,128)} %bitcast.3), custom_call_target="tpu_custom_call" | custom-call | tf_op jit(solution)/shard_map/propagate/pallas_call | solution.py:309
  120.7 1.3 %copy.6 = f32[1,2,128,2048]{3,2,1,0:T(8,128)} copy(f32[1,2,128,2048]{3,2,1,0:T(8,128)S(1)} %bitcast.2) | data formatting | bytes 4194304
